TPU v7x, 256 devices: a whole 4x4x8 slice. The times are simulated.
256 devices in a mesh: section: 8 (over x, core), blk: 32 (over y, z).
Axes of the slice: x: 4, y: 4, z: 8, core: 2. Of those that a mesh axis runs over, the one named last changes fastest.
Arguments:
- hidden: bfloat16 [16384, 1536], P('blk'), may hold values from -6 to 6
- stale_kv: bfloat16 [8, 16384, 3072], P('section', 'blk'), may hold values from -6 to 6
- w_qkv: bfloat16 [8, 1536, 4608], P('section', 'blk'), may hold values from -0.15625 to 0.15625
- w_out: bfloat16 [8, 1536, 1536], P('section', 'blk'), may hold values from -0.15625 to 0.15625
- q_gain: float32 [8, 128], P('section'), may hold values from 0.25 to 1.75
- k_gain: float32 [8, 128], P('section'), may hold values from 0.25 to 1.75
- mod_table: float32 [8, 16, 3, 1536], P('section'), may hold values from -4 to 4
- pattern: int32 [128, 8], P('blk'), may hold values from 0 to 1, as said below
- step_index: int32 [128], P('blk'), may hold values from 0 to 15
- order: int32 [4], replicated, may hold values from 0 to 3, each once
Outputs:
- layer_out: bfloat16 [8, 16384, 1536], P('section', 'blk')
- kv_cache: bfloat16 [8, 16384, 3072], P('section', 'blk')
Inputs may be any that keep to these rules, and one draw needn't show every extreme that they name: `pattern`: every row of the query tile's own tile (candidate c = tile index mod 4) is 1. `order`: names each patch once.
All inputs are finite; a program needn't handle non-finite values.
Results may differ from a plain program's by a relative error of at most 0.01.
Values may be sent and summed in bfloat16 or wider, within the bound.
A program may use at most 128 MiB of HBM per device.

v0:
```python
import math
import jax
import jax.numpy as jnp
from jax import lax
from jax.sharding import PartitionSpec as P

D = 1536
HEADS = 12
HDIM = 128
TILE = 128
PATCHES = 4
TSTEPS = 16
TOK_DEV = 128
NORM_EPS = 1e-06


def shifted(value, axis, steps):
    count = lax.axis_size(axis)
    pairs = [(source, (source + steps) % count) for source in range(count)]
    return lax.ppermute(value, axis, pairs)


def shifted_2(x, axis, by):
    count = lax.axis_size(axis)
    pairs = [(i, i + by) for i in range(count) if 0 <= i + by < count]
    return lax.ppermute(x, axis, pairs)


def layer_norm(values):
    centre = values - jnp.mean(values, axis=-1, keepdims=True)
    spread = jnp.mean(centre * centre, axis=-1, keepdims=True)
    return centre * lax.rsqrt(spread + NORM_EPS)


def head_norm(values, gain_row):
    square = jnp.mean(values * values, axis=-1, keepdims=True)
    return values * lax.rsqrt(square + NORM_EPS) * gain_row


def on_device(
    hidden, stale_kv, w_qkv, w_out, q_gain, k_gain, mod_table, pattern, step_index, order
):
    inner_width = HEADS * HDIM
    rows_patch = TOK_DEV
    tiles_patch = rows_patch // TILE
    candidate_tiles = pattern.shape[1]
    sections = lax.axis_size("section")
    section_id = lax.axis_index("section")
    full_qkv, full_out = (
        lax.all_gather(w_qkv[0], "blk", axis=0, tiled=True),
        lax.all_gather(w_out[0], "blk", axis=0, tiled=True),
    )
    query_gain = q_gain[0]
    key_gain = k_gain[0]
    modulation_table = mod_table[0].reshape(TSTEPS, 3 * D)
    tile_masks = pattern.reshape(PATCHES, tiles_patch, candidate_tiles)
    steps_tiles = step_index.reshape(PATCHES, tiles_patch)
    input_rows = hidden.reshape(PATCHES, rows_patch, D)
    own_store = stale_kv[0].reshape(PATCHES, rows_patch, 2 * inner_width)
    near_store = shifted(own_store, "blk", 1)
    received = jnp.zeros((rows_patch, D), jnp.bfloat16)
    results = jnp.zeros((PATCHES, rows_patch, D), jnp.bfloat16)
    inverse_root = 1.0 / math.sqrt(HDIM)

    def slot_step(slot, state_now):
        received, own_store, near_store, results = state_now
        offset = slot - section_id
        active = jnp.logical_and(offset >= 0, offset < PATCHES)
        clipped = jnp.clip(offset, 0, PATCHES - 1)
        patch_id = jnp.sum(jnp.where(jnp.arange(PATCHES) == clipped, order, 0))
        tokens = jnp.where(
            section_id == 0,
            lax.dynamic_index_in_dim(input_rows, patch_id, 0, keepdims=False),
            received,
        )
        tile_steps = lax.dynamic_index_in_dim(steps_tiles, patch_id, 0, keepdims=False)
        one_hot = (tile_steps[:, None] == jnp.arange(TSTEPS)[None, :]).astype(jnp.float32)
        modulation = jnp.dot(one_hot, modulation_table, precision=lax.Precision.HIGHEST)
        modulation = jnp.broadcast_to(modulation[:, None, :], (tiles_patch, TILE, 3 * D)).reshape(
            rows_patch, 3 * D
        )
        shift_term = modulation[:, :D]
        scale_term = modulation[:, D : 2 * D]
        gate_term = modulation[:, 2 * D :]

        def project(token_rows):
            modulated = (
                layer_norm(token_rows.astype(jnp.float32)) * (1.0 + scale_term) + shift_term
            ).astype(jnp.bfloat16)
            qkv = jnp.dot(modulated, full_qkv, preferred_element_type=jnp.float32)
            queries = head_norm(
                qkv[:, :inner_width].reshape(rows_patch, HEADS, HDIM), query_gain
            ).astype(jnp.bfloat16)
            return (modulated, queries, qkv[:, inner_width:].astype(jnp.bfloat16))

        def spare_project(token_rows):
            return (
                jnp.zeros((rows_patch, D), jnp.bfloat16),
                jnp.zeros((rows_patch, HEADS, HDIM), jnp.bfloat16),
                jnp.zeros((rows_patch, 2 * inner_width), jnp.bfloat16),
            )

        modulated, queries, fresh_kv = lax.cond(active, project, spare_project, tokens)
        own_store = jnp.where(
            active, lax.dynamic_update_index_in_dim(own_store, fresh_kv, patch_id, 0), own_store
        )
        near_fresh = shifted(fresh_kv, "blk", 1)
        near_store = jnp.where(
            active, lax.dynamic_update_index_in_dim(near_store, near_fresh, patch_id, 0), near_store
        )
        tile_mask = lax.dynamic_index_in_dim(tile_masks, patch_id, 0, keepdims=False)

        def attend(operands):
            token_rows, query_rows, own_rows, near_rows = operands
            candidates = jnp.concatenate(
                [own_rows.reshape(-1, 2 * inner_width), near_rows.reshape(-1, 2 * inner_width)],
                axis=0,
            )
            key_rows = head_norm(
                candidates[:, :inner_width].astype(jnp.float32).reshape(-1, HEADS, HDIM), key_gain
            ).astype(jnp.bfloat16)
            value_rows = candidates[:, inner_width:].reshape(-1, HEADS, HDIM)
            token_mask = jnp.broadcast_to(
                tile_mask.astype(jnp.float32)[:, None, :, None],
                (tiles_patch, TILE, candidate_tiles, TILE),
            ).reshape(rows_patch, candidate_tiles * TILE)
            scores = (
                jnp.einsum("qhd,khd->hqk", query_rows, key_rows, preferred_element_type=jnp.float32)
                * inverse_root
            )
            expo = jnp.exp(scores) * token_mask[None]
            weight_sum = jnp.sum(expo, axis=-1)
            mixture = jnp.einsum(
                "hqk,khd->qhd",
                expo.astype(jnp.bfloat16),
                value_rows,
                preferred_element_type=jnp.float32,
            )
            attended = (
                (mixture / jnp.transpose(weight_sum)[:, :, None])
                .reshape(rows_patch, inner_width)
                .astype(jnp.bfloat16)
            )
            projected = jnp.dot(attended, full_out, preferred_element_type=jnp.float32)
            return (token_rows.astype(jnp.float32) + gate_term * projected).astype(jnp.bfloat16)

        def spare_attend(operands):
            return jnp.zeros((rows_patch, D), jnp.bfloat16)

        output_rows = lax.cond(
            active, attend, spare_attend, (tokens, queries, own_store, near_store)
        )
        results = jnp.where(
            active, lax.dynamic_update_index_in_dim(results, output_rows, patch_id, 0), results
        )
        received = shifted_2(output_rows, "section", 1)
        return (received, own_store, near_store, results)

    slot_count = PATCHES + sections - 1
    received, own_store, near_store, results = lax.fori_loop(
        0, slot_count, slot_step, (received, own_store, near_store, results)
    )
    layer_out = results.reshape(1, PATCHES * rows_patch, D)
    kv_cache = own_store.reshape(1, PATCHES * rows_patch, 2 * inner_width)
    return (layer_out, kv_cache)


def solution(mesh):
    in_specs = (
        P("blk", None),
        P("section", "blk", None),
        P("section", "blk", None),
        P("section", "blk", None),
        P("section", None),
        P("section", None),
        P("section", None, None, None),
        P("blk", None),
        P("blk"),
        P(),
    )
    out_specs = (P("section", "blk", None), P("section", "blk", None))
    return jax.shard_map(
        on_device, mesh=mesh, in_specs=in_specs, out_specs=out_specs, check_vma=False
    )
```

profile of v0, /device:TPU:7, one launch (start us, length us, event | category | flops | bytes accessed | tf_op | source)
XLA Modules:
  0.0 1030.1 jit_solution(15740919164373035649)
XLA Ops:
  7.2 3.8 copy.63
  14.6 101.2 %collective-permute-done.2 = bf16[4,128,3072]{2,1,0:T(8,128)(2,1)} collective-permute-done((bf16[4,128,3072]{2,1,0:T(8,128)(2,1)}, bf16[4,128,3072]{2,1,0:T(8,128)(2,1)}, u32[]{:S(2)}, u32[]{:S(2)}) %collective-permute-start.2) | collective-permute-done | bytes 3145760 | tf_op jit(solution)/shard_map/ppermute | solution.py:20
  115.7 125.9 %all-gather.5.cloned.1.call-done = bf16[1,1536,4608]{2,1,0:T(8,128)(2,1)} async-done(((bf16[1,48,4608]{2,1,0:T(8,128)(2,1)}), bf16[1,1536,4608]{2,1,0:T(8,128)(2,1)}) %all-gather.5.cloned.1.call-update) | async-done | bytes 14155792 | tf_op jit(solution)/shard_map/all_gather | solution.py:50
  242.9 780.4 %while.20 = (s32[]{:T(128)}, bf16[128,1536]{1,0:T(8,128)(2,1)S(1)}, bf16[4,128,3072]{2,1,0:T(8,128)(2,1)}, bf16[4,128,3072]{2,1,0:T(8,128)(2,1)}, bf16[4,128,153...) while((s32[]{:T(128)}, bf16[128,1536]{1,0:T(8,128)(2,1)S(1)}, ...), condition=%wide.region_11.12_spmd, body=%wide.region_0.11_spmd.sunk | while | flops 3260855808 | bytes 107183792 | solution.py:160
  254.6 19.3 %collective-permute-done = bf16[128,3072]{1,0:T(8,128)(2,1)S(1)} collective-permute-done((bf16[128,3072]{1,0:T(8,128)(2,1)}, bf16[128,3072]{1,0:T(8,128)(2,1)S(1)}, u32[]{:S(2)}, u32[]{:S(2)}) %collective-permute-start) | collective-permute-done | bytes 786464 | tf_op jit(solution)/shard_map/while/body/eval_jaxpr/ppermute | solution.py:20
  294.6 14.4 %collective-permute-done = bf16[128,3072]{1,0:T(8,128)(2,1)S(1)} collective-permute-done((bf16[128,3072]{1,0:T(8,128)(2,1)}, bf16[128,3072]{1,0:T(8,128)(2,1)S(1)}, u32[]{:S(2)}, u32[]{:S(2)}) %collective-permute-start) | collective-permute-done | bytes 786464 | tf_op jit(solution)/shard_map/while/body/eval_jaxpr/ppermute | solution.py:20
  315.9 7.1 collective-permute-done.1
  334.6 13.3 %collective-permute-done = bf16[128,3072]{1,0:T(8,128)(2,1)S(1)} collective-permute-done((bf16[128,3072]{1,0:T(8,128)(2,1)}, bf16[128,3072]{1,0:T(8,128)(2,1)S(1)}, u32[]{:S(2)}, u32[]{:S(2)}) %collective-permute-start) | collective-permute-done | bytes 786464 | tf_op jit(solution)/shard_map/while/body/eval_jaxpr/ppermute | solution.py:20
  354.8 8.2 collective-permute-done.1
  374.6 14.4 %collective-permute-done = bf16[128,3072]{1,0:T(8,128)(2,1)S(1)} collective-permute-done((bf16[128,3072]{1,0:T(8,128)(2,1)}, bf16[128,3072]{1,0:T(8,128)(2,1)S(1)}, u32[]{:S(2)}, u32[]{:S(2)}) %collective-permute-start) | collective-permute-done | bytes 786464 | tf_op jit(solution)/shard_map/while/body/eval_jaxpr/ppermute | solution.py:20
  395.9 7.1 collective-permute-done.1
  414.6 14.4 %collective-permute-done = bf16[128,3072]{1,0:T(8,128)(2,1)S(1)} collective-permute-done((bf16[128,3072]{1,0:T(8,128)(2,1)}, bf16[128,3072]{1,0:T(8,128)(2,1)S(1)}, u32[]{:S(2)}, u32[]{:S(2)}) %collective-permute-start) | collective-permute-done | bytes 786464 | tf_op jit(solution)/shard_map/while/body/eval_jaxpr/ppermute | solution.py:20
  435.9 7.1 collective-permute-done.1
  454.6 14.4 %collective-permute-done = bf16[128,3072]{1,0:T(8,128)(2,1)S(1)} collective-permute-done((bf16[128,3072]{1,0:T(8,128)(2,1)}, bf16[128,3072]{1,0:T(8,128)(2,1)S(1)}, u32[]{:S(2)}, u32[]{:S(2)}) %collective-permute-start) | collective-permute-done | bytes 786464 | tf_op jit(solution)/shard_map/while/body/eval_jaxpr/ppermute | solution.py:20
  475.9 7.1 collective-permute-done.1
  494.6 12.2 %collective-permute-done = bf16[128,3072]{1,0:T(8,128)(2,1)S(1)} collective-permute-done((bf16[128,3072]{1,0:T(8,128)(2,1)}, bf16[128,3072]{1,0:T(8,128)(2,1)S(1)}, u32[]{:S(2)}, u32[]{:S(2)}) %collective-permute-start) | collective-permute-done | bytes 786464 | tf_op jit(solution)/shard_map/while/body/eval_jaxpr/ppermute | solution.py:20
  513.7 209.5 %collective-permute-done.1 = bf16[128,1536]{1,0:T(8,128)(2,1)S(1)} collective-permute-done((bf16[128,1536]{1,0:T(8,128)(2,1)}, bf16[128,1536]{1,0:T(8,128)(2,1)S(1)}, u32[]{:S(2)}, u32[]{:S(2)}) %collective-permute-start.1) | collective-permute-done | bytes 393248 | tf_op jit(solution)/shard_map/while/body/eval_jaxpr/ppermute | solution.py:26
  729.7 13.7 %conditional.4 = (bf16[128,12,128]{0,2,1:T(8,128)(2,1)}, bf16[128,3072]{1,0:T(8,128)(2,1)}, bf16[1,128,3072]{2,1,0:T(8,128)(2,1)}) conditional(s32[]{:T(128)} %convert_element_type.92, () %tuple.70, (bf16[128,1536]{1,0:T(8,128)(2,1)S(1)}, f32[4608]{0:T(1024)}, bf16[1536,4608]{1,0:T(8,128)(2,1)}, f32[1,128]{1,0:T(1,128)S(1)}) %tuple.71), branch_computations={%region_2.2_spmd, %region_3.6_spmd} | conditional | flops 1815284864 | bytes 26018840 | solution.py:103
  730.9 7.1 fusion.6
  745.9 11.9 %collective-permute-done = bf16[128,3072]{1,0:T(8,128)(2,1)S(1)} collective-permute-done((bf16[128,3072]{1,0:T(8,128)(2,1)}, bf16[128,3072]{1,0:T(8,128)(2,1)S(1)}, u32[]{:S(2)}, u32[]{:S(2)}) %collective-permute-start) | collective-permute-done | bytes 786464 | tf_op jit(solution)/shard_map/while/body/eval_jaxpr/ppermute | solution.py:20
  760.1 24.4 %conditional.5 = (bf16[128,1536]{1,0:T(8,128)(2,1)}, bf16[1,128,1536]{2,1,0:T(8,128)(2,1)}) conditional(s32[]{:T(128)} %convert_element_type.92, () %tuple.69, (bf16[128,1536]{1,0:T(8,128)(2,1)S(1)}, f32[4608]{0:T(1024)}, bf16[4,128,3072]{2,1,0:T(8,128)(2,1)}, bf16[4,128,3072]{2,1,0:T(8,128)(2,1)}, f32[1,128]{1,0:T(1,128)S(1)}, ...), branch_computations={%region_7.7_spmd, %region_8.10_spmd} | conditional | flops 1443506688 | bytes 69053088 | solution.py:150
  763.3 4.7 copy.31
  768.0 5.6 pad_maximum_fusion
  775.2 3.3 bitcast_reduce_fusion
  787.7 10.2 collective-permute-done.1
  804.5 13.7 %conditional.4 = (bf16[128,12,128]{0,2,1:T(8,128)(2,1)}, bf16[128,3072]{1,0:T(8,128)(2,1)}, bf16[1,128,3072]{2,1,0:T(8,128)(2,1)}) conditional(s32[]{:T(128)} %convert_element_type.92, () %tuple.70, (bf16[128,1536]{1,0:T(8,128)(2,1)S(1)}, f32[4608]{0:T(1024)}, bf16[1536,4608]{1,0:T(8,128)(2,1)}, f32[1,128]{1,0:T(1,128)S(1)}) %tuple.71), branch_computations={%region_2.2_spmd, %region_3.6_spmd} | conditional | flops 1815284864 | bytes 26018840 | solution.py:103
  805.7 7.1 fusion.6
  820.7 11.9 %collective-permute-done = bf16[128,3072]{1,0:T(8,128)(2,1)S(1)} collective-permute-done((bf16[128,3072]{1,0:T(8,128)(2,1)}, bf16[128,3072]{1,0:T(8,128)(2,1)S(1)}, u32[]{:S(2)}, u32[]{:S(2)}) %collective-permute-start) | collective-permute-done | bytes 786464 | tf_op jit(solution)/shard_map/while/body/eval_jaxpr/ppermute | solution.py:20
  834.8 24.4 %conditional.5 = (bf16[128,1536]{1,0:T(8,128)(2,1)}, bf16[1,128,1536]{2,1,0:T(8,128)(2,1)}) conditional(s32[]{:T(128)} %convert_element_type.92, () %tuple.69, (bf16[128,1536]{1,0:T(8,128)(2,1)S(1)}, f32[4608]{0:T(1024)}, bf16[4,128,3072]{2,1,0:T(8,128)(2,1)}, bf16[4,128,3072]{2,1,0:T(8,128)(2,1)}, f32[1,128]{1,0:T(1,128)S(1)}, ...), branch_computations={%region_7.7_spmd, %region_8.10_spmd} | conditional | flops 1443506688 | bytes 69053088 | solution.py:150
  838.0 4.7 copy.31
  842.8 5.6 pad_maximum_fusion
  849.9 3.3 bitcast_reduce_fusion
  862.5 12.3 %collective-permute-done.1 = bf16[128,1536]{1,0:T(8,128)(2,1)S(1)} collective-permute-done((bf16[128,1536]{1,0:T(8,128)(2,1)}, bf16[128,1536]{1,0:T(8,128)(2,1)S(1)}, u32[]{:S(2)}, u32[]{:S(2)}) %collective-permute-start.1) | collective-permute-done | bytes 393248 | tf_op jit(solution)/shard_map/while/body/eval_jaxpr/ppermute | solution.py:26
  881.4 13.7 %conditional.4 = (bf16[128,12,128]{0,2,1:T(8,128)(2,1)}, bf16[128,3072]{1,0:T(8,128)(2,1)}, bf16[1,128,3072]{2,1,0:T(8,128)(2,1)}) conditional(s32[]{:T(128)} %convert_element_type.92, () %tuple.70, (bf16[128,1536]{1,0:T(8,128)(2,1)S(1)}, f32[4608]{0:T(1024)}, bf16[1536,4608]{1,0:T(8,128)(2,1)}, f32[1,128]{1,0:T(1,128)S(1)}) %tuple.71), branch_computations={%region_2.2_spmd, %region_3.6_spmd} | conditional | flops 1815284864 | bytes 26018840 | solution.py:103
  882.6 7.2 fusion.6
  897.6 11.9 %collective-permute-done = bf16[128,3072]{1,0:T(8,128)(2,1)S(1)} collective-permute-done((bf16[128,3072]{1,0:T(8,128)(2,1)}, bf16[128,3072]{1,0:T(8,128)(2,1)S(1)}, u32[]{:S(2)}, u32[]{:S(2)}) %collective-permute-start) | collective-permute-done | bytes 786464 | tf_op jit(solution)/shard_map/while/body/eval_jaxpr/ppermute | solution.py:20
  911.7 24.4 %conditional.5 = (bf16[128,1536]{1,0:T(8,128)(2,1)}, bf16[1,128,1536]{2,1,0:T(8,128)(2,1)}) conditional(s32[]{:T(128)} %convert_element_type.92, () %tuple.69, (bf16[128,1536]{1,0:T(8,128)(2,1)S(1)}, f32[4608]{0:T(1024)}, bf16[4,128,3072]{2,1,0:T(8,128)(2,1)}, bf16[4,128,3072]{2,1,0:T(8,128)(2,1)}, f32[1,128]{1,0:T(1,128)S(1)}, ...), branch_computations={%region_7.7_spmd, %region_8.10_spmd} | conditional | flops 1443506688 | bytes 69053088 | solution.py:150
  914.9 4.7 copy.31
  919.7 5.6 pad_maximum_fusion
  926.8 3.3 bitcast_reduce_fusion
  939.4 14.8 %collective-permute-done.1 = bf16[128,1536]{1,0:T(8,128)(2,1)S(1)} collective-permute-done((bf16[128,1536]{1,0:T(8,128)(2,1)}, bf16[128,1536]{1,0:T(8,128)(2,1)S(1)}, u32[]{:S(2)}, u32[]{:S(2)}) %collective-permute-start.1) | collective-permute-done | bytes 393248 | tf_op jit(solution)/shard_map/while/body/eval_jaxpr/ppermute | solution.py:26
  960.8 13.7 %conditional.4 = (bf16[128,12,128]{0,2,1:T(8,128)(2,1)}, bf16[128,3072]{1,0:T(8,128)(2,1)}, bf16[1,128,3072]{2,1,0:T(8,128)(2,1)}) conditional(s32[]{:T(128)} %convert_element_type.92, () %tuple.70, (bf16[128,1536]{1,0:T(8,128)(2,1)S(1)}, f32[4608]{0:T(1024)}, bf16[1536,4608]{1,0:T(8,128)(2,1)}, f32[1,128]{1,0:T(1,128)S(1)}) %tuple.71), branch_computations={%region_2.2_spmd, %region_3.6_spmd} | conditional | flops 1815284864 | bytes 26018840 | solution.py:103
  962.0 7.1 fusion.6
  977.0 15.9 %collective-permute-done = bf16[128,3072]{1,0:T(8,128)(2,1)S(1)} collective-permute-done((bf16[128,3072]{1,0:T(8,128)(2,1)}, bf16[128,3072]{1,0:T(8,128)(2,1)S(1)}, u32[]{:S(2)}, u32[]{:S(2)}) %collective-permute-start) | collective-permute-done | bytes 786464 | tf_op jit(solution)/shard_map/while/body/eval_jaxpr/ppermute | solution.py:20
  995.1 24.4 %conditional.5 = (bf16[128,1536]{1,0:T(8,128)(2,1)}, bf16[1,128,1536]{2,1,0:T(8,128)(2,1)}) conditional(s32[]{:T(128)} %convert_element_type.92, () %tuple.69, (bf16[128,1536]{1,0:T(8,128)(2,1)S(1)}, f32[4608]{0:T(1024)}, bf16[4,128,3072]{2,1,0:T(8,128)(2,1)}, bf16[4,128,3072]{2,1,0:T(8,128)(2,1)}, f32[1,128]{1,0:T(1,128)S(1)}, ...), branch_computations={%region_7.7_spmd, %region_8.10_spmd} | conditional | flops 1443506688 | bytes 69053088 | solution.py:150
  998.3 4.7 copy.31
  1003.0 5.6 pad_maximum_fusion
  1010.1 3.3 bitcast_reduce_fusion
  (274 shorter events, 274.5 us)
Async XLA Ops:
  7.2 6.4 copy-start
  7.2 108.6 %all-gather.7.cloned.1.call-start = ((), (), s32[]{:S(2)}) async-start(), calls=%async_computation.1 | async-start | bytes 4866048 | tf_op jit(solution)/shard_map/all_gather | solution.py:51
  11.0 231.9 %copy-start.1 = (f32[1,128]{1,0:T(1,128)S(1)}, f32[1,128]{1,0:T(1,128)}, u32[]{:S(2)}) copy-start(f32[1,128]{1,0:T(1,128)} %param.20) | copy-start | bytes 1540
  11.0 231.9 %copy-start.2 = (s32[4]{0:T(128)S(1)}, s32[4]{0:T(128)}, u32[]{:S(2)}) copy-start(s32[4]{0:T(128)} %param.25) | copy-start | bytes 52
  11.0 231.9 %copy-start.3 = (s32[4]{0:T(128)S(1)}, s32[4]{0:T(128)}, u32[]{:S(2)}) copy-start(s32[4]{0:T(128)} %param.24) | copy-start | bytes 52
  11.0 231.9 %copy-start.4 = (f32[1,128]{1,0:T(1,128)S(1)}, f32[1,128]{1,0:T(1,128)}, u32[]{:S(2)}) copy-start(f32[1,128]{1,0:T(1,128)} %param.21) | copy-start | bytes 1540
  11.0 230.5 %all-gather.5.cloned.1.call-start = ((), (), s32[]{:S(2)}) async-start(), calls=%async_computation | async-start | bytes 14598144 | tf_op jit(solution)/shard_map/all_gather | solution.py:50
  11.8 103.9 %collective-permute-start.2 = (bf16[4,128,3072]{2,1,0:T(8,128)(2,1)}, bf16[4,128,3072]{2,1,0:T(8,128)(2,1)}, u32[]{:S(2)}, u32[]{:S(2)}) collective-permute-start(bf16[4,128,3072]{2,1,0:T(8,128)(2,1)} %bitcast.20), channel_id=1, source_target_pairs={{0,1},{1,2},{2,3},{3,4},{4,5},{5,6},{6,7},{7,8},{8,9},{9,10},{10,1... | collective-permute-start | bytes 9437192 | tf_op jit(solution)/shard_map/ppermute | solution.py:20
  252.4 21.5 %collective-permute-start = (bf16[128,3072]{1,0:T(8,128)(2,1)}, bf16[128,3072]{1,0:T(8,128)(2,1)S(1)}, u32[]{:S(2)}, u32[]{:S(2)}) collective-permute-start(bf16[128,3072]{1,0:T(8,128)(2,1)} %get-tuple-element.585), channel_id=1, source_target_pairs={{0,1},{1,2},{2,3},{3,4},{4,5},{5,6},{6,7},{7,8},{8,9},{9,10},{10,1... | collective-permute-start | bytes 2359304 | tf_op jit(solution)/shard_map/while/body/eval_jaxpr/ppermute | solution.py:20
  277.7 5.3 collective-permute-start.1
  292.4 16.6 %collective-permute-start = (bf16[128,3072]{1,0:T(8,128)(2,1)}, bf16[128,3072]{1,0:T(8,128)(2,1)S(1)}, u32[]{:S(2)}, u32[]{:S(2)}) collective-permute-start(bf16[128,3072]{1,0:T(8,128)(2,1)} %get-tuple-element.585), channel_id=1, source_target_pairs={{0,1},{1,2},{2,3},{3,4},{4,5},{5,6},{6,7},{7,8},{8,9},{9,10},{10,1... | collective-permute-start | bytes 2359304 | tf_op jit(solution)/shard_map/while/body/eval_jaxpr/ppermute | solution.py:20
  312.7 10.2 collective-permute-start.1
  332.4 15.5 %collective-permute-start = (bf16[128,3072]{1,0:T(8,128)(2,1)}, bf16[128,3072]{1,0:T(8,128)(2,1)S(1)}, u32[]{:S(2)}, u32[]{:S(2)}) collective-permute-start(bf16[128,3072]{1,0:T(8,128)(2,1)} %get-tuple-element.585), channel_id=1, source_target_pairs={{0,1},{1,2},{2,3},{3,4},{4,5},{5,6},{6,7},{7,8},{8,9},{9,10},{10,1... | collective-permute-start | bytes 2359304 | tf_op jit(solution)/shard_map/while/body/eval_jaxpr/ppermute | solution.py:20
  351.6 11.3 %collective-permute-start.1 = (bf16[128,1536]{1,0:T(8,128)(2,1)}, bf16[128,1536]{1,0:T(8,128)(2,1)S(1)}, u32[]{:S(2)}, u32[]{:S(2)}) collective-permute-start(bf16[128,1536]{1,0:T(8,128)(2,1)} %get-tuple-element.587), channel_id=1, source_target_pairs={{0,32},{32,64},{64,96},{96,128},{128,160},{160,192},{192,224},{1,3... | collective-permute-start | bytes 1179656 | tf_op jit(solution)/shard_map/while/body/eval_jaxpr/ppermute | solution.py:26
  372.4 16.6 %collective-permute-start = (bf16[128,3072]{1,0:T(8,128)(2,1)}, bf16[128,3072]{1,0:T(8,128)(2,1)S(1)}, u32[]{:S(2)}, u32[]{:S(2)}) collective-permute-start(bf16[128,3072]{1,0:T(8,128)(2,1)} %get-tuple-element.585), channel_id=1, source_target_pairs={{0,1},{1,2},{2,3},{3,4},{4,5},{5,6},{6,7},{7,8},{8,9},{9,10},{10,1... | collective-permute-start | bytes 2359304 | tf_op jit(solution)/shard_map/while/body/eval_jaxpr/ppermute | solution.py:20
  392.7 10.2 collective-permute-start.1
  412.4 16.6 %collective-permute-start = (bf16[128,3072]{1,0:T(8,128)(2,1)}, bf16[128,3072]{1,0:T(8,128)(2,1)S(1)}, u32[]{:S(2)}, u32[]{:S(2)}) collective-permute-start(bf16[128,3072]{1,0:T(8,128)(2,1)} %get-tuple-element.585), channel_id=1, source_target_pairs={{0,1},{1,2},{2,3},{3,4},{4,5},{5,6},{6,7},{7,8},{8,9},{9,10},{10,1... | collective-permute-start | bytes 2359304 | tf_op jit(solution)/shard_map/while/body/eval_jaxpr/ppermute | solution.py:20
  432.7 10.2 collective-permute-start.1
  452.4 16.6 %collective-permute-start = (bf16[128,3072]{1,0:T(8,128)(2,1)}, bf16[128,3072]{1,0:T(8,128)(2,1)S(1)}, u32[]{:S(2)}, u32[]{:S(2)}) collective-permute-start(bf16[128,3072]{1,0:T(8,128)(2,1)} %get-tuple-element.585), channel_id=1, source_target_pairs={{0,1},{1,2},{2,3},{3,4},{4,5},{5,6},{6,7},{7,8},{8,9},{9,10},{10,1... | collective-permute-start | bytes 2359304 | tf_op jit(solution)/shard_map/while/body/eval_jaxpr/ppermute | solution.py:20
  472.7 10.2 collective-permute-start.1
  492.4 14.4 %collective-permute-start = (bf16[128,3072]{1,0:T(8,128)(2,1)}, bf16[128,3072]{1,0:T(8,128)(2,1)S(1)}, u32[]{:S(2)}, u32[]{:S(2)}) collective-permute-start(bf16[128,3072]{1,0:T(8,128)(2,1)} %get-tuple-element.585), channel_id=1, source_target_pairs={{0,1},{1,2},{2,3},{3,4},{4,5},{5,6},{6,7},{7,8},{8,9},{9,10},{10,1... | collective-permute-start | bytes 2359304 | tf_op jit(solution)/shard_map/while/body/eval_jaxpr/ppermute | solution.py:20
  510.5 212.6 %collective-permute-start.1 = (bf16[128,1536]{1,0:T(8,128)(2,1)}, bf16[128,1536]{1,0:T(8,128)(2,1)S(1)}, u32[]{:S(2)}, u32[]{:S(2)}) collective-permute-start(bf16[128,1536]{1,0:T(8,128)(2,1)} %get-tuple-element.587), channel_id=1, source_target_pairs={{0,32},{32,64},{64,96},{96,128},{128,160},{160,192},{192,224},{1,3... | collective-permute-start | bytes 1179656 | tf_op jit(solution)/shard_map/while/body/eval_jaxpr/ppermute | solution.py:26
  743.5 14.4 %collective-permute-start = (bf16[128,3072]{1,0:T(8,128)(2,1)}, bf16[128,3072]{1,0:T(8,128)(2,1)S(1)}, u32[]{:S(2)}, u32[]{:S(2)}) collective-permute-start(bf16[128,3072]{1,0:T(8,128)(2,1)} %get-tuple-element.585), channel_id=1, source_target_pairs={{0,1},{1,2},{2,3},{3,4},{4,5},{5,6},{6,7},{7,8},{8,9},{9,10},{10,1... | collective-permute-start | bytes 2359304 | tf_op jit(solution)/shard_map/while/body/eval_jaxpr/ppermute | solution.py:20
  775.1 6.0 slice-start
  778.5 2.7 slice-start.1
  784.5 13.5 %collective-permute-start.1 = (bf16[128,1536]{1,0:T(8,128)(2,1)}, bf16[128,1536]{1,0:T(8,128)(2,1)S(1)}, u32[]{:S(2)}, u32[]{:S(2)}) collective-permute-start(bf16[128,1536]{1,0:T(8,128)(2,1)} %get-tuple-element.587), channel_id=1, source_target_pairs={{0,32},{32,64},{64,96},{96,128},{128,160},{160,192},{192,224},{1,3... | collective-permute-start | bytes 1179656 | tf_op jit(solution)/shard_map/while/body/eval_jaxpr/ppermute | solution.py:26
  818.3 14.4 %collective-permute-start = (bf16[128,3072]{1,0:T(8,128)(2,1)}, bf16[128,3072]{1,0:T(8,128)(2,1)S(1)}, u32[]{:S(2)}, u32[]{:S(2)}) collective-permute-start(bf16[128,3072]{1,0:T(8,128)(2,1)} %get-tuple-element.585), channel_id=1, source_target_pairs={{0,1},{1,2},{2,3},{3,4},{4,5},{5,6},{6,7},{7,8},{8,9},{9,10},{10,1... | collective-permute-start | bytes 2359304 | tf_op jit(solution)/shard_map/while/body/eval_jaxpr/ppermute | solution.py:20
  849.9 6.0 slice-start
  853.2 2.7 slice-start.1
  859.3 15.6 %collective-permute-start.1 = (bf16[128,1536]{1,0:T(8,128)(2,1)}, bf16[128,1536]{1,0:T(8,128)(2,1)S(1)}, u32[]{:S(2)}, u32[]{:S(2)}) collective-permute-start(bf16[128,1536]{1,0:T(8,128)(2,1)} %get-tuple-element.587), channel_id=1, source_target_pairs={{0,32},{32,64},{64,96},{96,128},{128,160},{160,192},{192,224},{1,3... | collective-permute-start | bytes 1179656 | tf_op jit(solution)/shard_map/while/body/eval_jaxpr/ppermute | solution.py:26
  895.2 14.4 %collective-permute-start = (bf16[128,3072]{1,0:T(8,128)(2,1)}, bf16[128,3072]{1,0:T(8,128)(2,1)S(1)}, u32[]{:S(2)}, u32[]{:S(2)}) collective-permute-start(bf16[128,3072]{1,0:T(8,128)(2,1)} %get-tuple-element.585), channel_id=1, source_target_pairs={{0,1},{1,2},{2,3},{3,4},{4,5},{5,6},{6,7},{7,8},{8,9},{9,10},{10,1... | collective-permute-start | bytes 2359304 | tf_op jit(solution)/shard_map/while/body/eval_jaxpr/ppermute | solution.py:20
  926.8 6.0 slice-start
  930.1 2.7 slice-start.1
  936.2 18.1 %collective-permute-start.1 = (bf16[128,1536]{1,0:T(8,128)(2,1)}, bf16[128,1536]{1,0:T(8,128)(2,1)S(1)}, u32[]{:S(2)}, u32[]{:S(2)}) collective-permute-start(bf16[128,1536]{1,0:T(8,128)(2,1)} %get-tuple-element.587), channel_id=1, source_target_pairs={{0,32},{32,64},{64,96},{96,128},{128,160},{160,192},{192,224},{1,3... | collective-permute-start | bytes 1179656 | tf_op jit(solution)/shard_map/while/body/eval_jaxpr/ppermute | solution.py:26
  974.5 18.3 %collective-permute-start = (bf16[128,3072]{1,0:T(8,128)(2,1)}, bf16[128,3072]{1,0:T(8,128)(2,1)S(1)}, u32[]{:S(2)}, u32[]{:S(2)}) collective-permute-start(bf16[128,3072]{1,0:T(8,128)(2,1)} %get-tuple-element.585), channel_id=1, source_target_pairs={{0,1},{1,2},{2,3},{3,4},{4,5},{5,6},{6,7},{7,8},{8,9},{9,10},{10,1... | collective-permute-start | bytes 2359304 | tf_op jit(solution)/shard_map/while/body/eval_jaxpr/ppermute | solution.py:20
  1010.1 6.0 slice-start
  1013.5 2.7 slice-start.1
  1019.5 3.8 collective-permute-start.1
Sparse Core Ops, SparseCore 0:
  11.2 102.6 all-gather.6
  116.4 125.1 all-gather.4
where the time goes:
time: 1030 us
  waiting for transfers between devices  668 us (65%)
  other arithmetic  126 us (12%)
  local copies, waits for them, and re-layouts  103 us (10%)
  matrix products  82.5 us (8%)
  loops' own time  20.9 us (2%)
  starting transfers between devices  15.9 us (2%)
  between operations  14.1 us (1%)
    ppermute x11, waiting for transfers between devices, shifted_2(): return lax.ppermute(x, axis, pairs)  286 us
    ppermute x12, waiting for transfers between devices, shifted(): return lax.ppermute(value, axis, pairs)  255 us
    all_gather x1, waiting for transfers between devices, on_device(): lax.all_gather(w_qkv[0], 'blk', axis=0, tiled=True)  126 us
    dot_general x4, matrix products, project(): qkv = jnp.dot(modulated, full_qkv, preferred_element_type=jnp.float32)  28.6 us
    dot_general x11, matrix products, slot_step(): jnp.dot(one_hot, modulation_table, precision=lax.Precision.HIGHEST)  26.6 us
    select_n x11, other arithmetic, slot_step(): jnp.where(active, lax.dynamic_update_index_in_dim(own_store, fresh_kv, pa...  25.1 us
    select_n x11, other arithmetic, slot_step(): jnp.where(active, lax.dynamic_update_index_in_dim(near_store, near_fresh,...  24.3 us
    concatenate x4, other arithmetic, attend(): jnp.concatenate([own_rows.reshape(-1, 2 * inner_width), near_rows.reshape...  22.5 us
  transfers between devices with their start and end apart: 25, of which 24 were waited for; matrix products, arithmetic and copies ran while one was open for 5% of the time, Pallas kernels for 0%

commit v1 on v0

--- a/solution.py
+++ b/solution.py
@@ -12,6 +12,14 @@
 TSTEPS = 16
 TOK_DEV = 128
 NORM_EPS = 1e-06
+
+
+def gather_from_all(array, axis, dim):
+    length = lax.axis_size(axis)
+    repeats = [length if d == dim else 1 for d in range(array.ndim)]
+    return lax.all_to_all(
+        jnp.tile(array, repeats), axis, split_axis=dim, concat_axis=dim, tiled=True
+    )
 
 
 def shifted(value, axis, steps):
@@ -47,7 +55,7 @@
     sections = lax.axis_size("section")
     section_id = lax.axis_index("section")
     full_qkv, full_out = (
-        lax.all_gather(w_qkv[0], "blk", axis=0, tiled=True),
+        gather_from_all(w_qkv[0], "blk", 0),
         lax.all_gather(w_out[0], "blk", axis=0, tiled=True),
     )
     query_gain = q_gain[0]

time: 1030 us -> 1240 us (1.20)
  waiting for transfers between devices: 668 us -> 843 us
  starting transfers between devices: 15.9 us -> 33.6 us
    ppermute x12, waiting for transfers between devices: 255 us -> 553 us  [shifted(): return lax.ppermute(value, axis, pairs)]
    all_gather x1 -> x0, waiting for transfers between devices: 126 us -> none  [on_device(): lax.all_gather(w_qkv[0], 'blk', axis=0, tiled=True)]
  transfers between devices with their start and end apart: 25 -> 25, of which waited for: 24 -> 23; matrix products, arithmetic and copies ran while one was open for 5% -> 4% of each run, Pallas kernels for 0% -> 0%
where the time goes in v1:
time: 1240 us; the launch traced here: 1230 us
  waiting for transfers between devices  843 us (68%)
  other arithmetic  126 us (10%)
  local copies, waits for them, and re-layouts  110 us (9%)
  matrix products  82.8 us (7%)
  starting transfers between devices  33.6 us (3%)
  loops' own time  23.8 us (2%)
  between operations  14.1 us (1%)
    ppermute x12, waiting for transfers between devices, shifted(): return lax.ppermute(value, axis, pairs)  553 us
    ppermute x11, waiting for transfers between devices, shifted_2(): return lax.ppermute(x, axis, pairs)  289 us
    dot_general x4, matrix products, project(): qkv = jnp.dot(modulated, full_qkv, preferred_element_type=jnp.float32)  28.6 us
    dot_general x11, matrix products, slot_step(): jnp.dot(one_hot, modulation_table, precision=lax.Precision.HIGHEST)  26.8 us
    select_n x11, other arithmetic, slot_step(): jnp.where(active, lax.dynamic_update_index_in_dim(own_store, fresh_kv, pa...  25.1 us
  transfers between devices with their start and end apart: 25, of which 23 were waited for; matrix products, arithmetic and copies ran while one was open for 4% of the time, Pallas kernels for 0%

profile of v1, /device:TPU:7, one launch (start us, length us, event | category | flops | bytes accessed | tf_op | source)
XLA Modules:
  0.0 1233.1 jit_solution(15838335971762245686)
XLA Ops:
  7.2 3.8 copy.63
  11.0 6.7 tile.9
  17.7 11.5 all-to-all-start
  32.2 406.2 %collective-permute-done.2 = bf16[4,128,3072]{2,1,0:T(8,128)(2,1)} collective-permute-done((bf16[4,128,3072]{2,1,0:T(8,128)(2,1)}, bf16[4,128,3072]{2,1,0:T(8,128)(2,1)}, u32[]{:S(2)}, u32[]{:S(2)}) %collective-permute-start.2) | collective-permute-done | bytes 3145760 | tf_op jit(solution)/shard_map/ppermute | solution.py:28
  439.7 786.5 %while.20 = (s32[]{:T(128)}, bf16[128,1536]{1,0:T(8,128)(2,1)S(1)}, bf16[4,128,3072]{2,1,0:T(8,128)(2,1)}, bf16[4,128,3072]{2,1,0:T(8,128)(2,1)}, bf16[4,128,153...) while((s32[]{:T(128)}, bf16[128,1536]{1,0:T(8,128)(2,1)S(1)}, ...), condition=%wide.region_11.12_spmd, body=%wide.region_0.11_spmd.sunk | while | flops 3260855808 | bytes 107183792 | solution.py:168
  451.9 18.9 %collective-permute-done = bf16[128,3072]{1,0:T(8,128)(2,1)S(1)} collective-permute-done((bf16[128,3072]{1,0:T(8,128)(2,1)}, bf16[128,3072]{1,0:T(8,128)(2,1)S(1)}, u32[]{:S(2)}, u32[]{:S(2)}) %collective-permute-start) | collective-permute-done | bytes 786464 | tf_op jit(solution)/shard_map/while/body/eval_jaxpr/ppermute | solution.py:28
  490.0 6.8 collective-permute-start
  499.0 7.1 collective-permute-done
  513.0 14.5 %collective-permute-done.1 = bf16[128,1536]{1,0:T(8,128)(2,1)S(1)} collective-permute-done((bf16[128,1536]{1,0:T(8,128)(2,1)}, bf16[128,1536]{1,0:T(8,128)(2,1)S(1)}, u32[]{:S(2)}, u32[]{:S(2)}) %collective-permute-start.1) | collective-permute-done | bytes 393248 | tf_op jit(solution)/shard_map/while/body/eval_jaxpr/ppermute | solution.py:34
  539.4 14.2 %collective-permute-done = bf16[128,3072]{1,0:T(8,128)(2,1)S(1)} collective-permute-done((bf16[128,3072]{1,0:T(8,128)(2,1)}, bf16[128,3072]{1,0:T(8,128)(2,1)S(1)}, u32[]{:S(2)}, u32[]{:S(2)}) %collective-permute-start) | collective-permute-done | bytes 786464 | tf_op jit(solution)/shard_map/while/body/eval_jaxpr/ppermute | solution.py:28
  560.4 7.3 collective-permute-done.1
  579.7 14.4 %collective-permute-done = bf16[128,3072]{1,0:T(8,128)(2,1)S(1)} collective-permute-done((bf16[128,3072]{1,0:T(8,128)(2,1)}, bf16[128,3072]{1,0:T(8,128)(2,1)S(1)}, u32[]{:S(2)}, u32[]{:S(2)}) %collective-permute-start) | collective-permute-done | bytes 786464 | tf_op jit(solution)/shard_map/while/body/eval_jaxpr/ppermute | solution.py:28
  601.0 7.1 collective-permute-done.1
  620.0 14.4 %collective-permute-done = bf16[128,3072]{1,0:T(8,128)(2,1)S(1)} collective-permute-done((bf16[128,3072]{1,0:T(8,128)(2,1)}, bf16[128,3072]{1,0:T(8,128)(2,1)S(1)}, u32[]{:S(2)}, u32[]{:S(2)}) %collective-permute-start) | collective-permute-done | bytes 786464 | tf_op jit(solution)/shard_map/while/body/eval_jaxpr/ppermute | solution.py:28
  641.3 7.1 collective-permute-done.1
  660.3 14.4 %collective-permute-done = bf16[128,3072]{1,0:T(8,128)(2,1)S(1)} collective-permute-done((bf16[128,3072]{1,0:T(8,128)(2,1)}, bf16[128,3072]{1,0:T(8,128)(2,1)S(1)}, u32[]{:S(2)}, u32[]{:S(2)}) %collective-permute-start) | collective-permute-done | bytes 786464 | tf_op jit(solution)/shard_map/while/body/eval_jaxpr/ppermute | solution.py:28
  681.6 7.1 collective-permute-done.1
  700.7 12.2 collective-permute-done
  719.8 205.2 %collective-permute-done.1 = bf16[128,1536]{1,0:T(8,128)(2,1)S(1)} collective-permute-done((bf16[128,1536]{1,0:T(8,128)(2,1)}, bf16[128,1536]{1,0:T(8,128)(2,1)S(1)}, u32[]{:S(2)}, u32[]{:S(2)}) %collective-permute-start.1) | collective-permute-done | bytes 393248 | tf_op jit(solution)/shard_map/while/body/eval_jaxpr/ppermute | solution.py:34
  931.8 13.7 %conditional.4 = (bf16[128,12,128]{0,2,1:T(8,128)(2,1)}, bf16[128,3072]{1,0:T(8,128)(2,1)}, bf16[1,128,3072]{2,1,0:T(8,128)(2,1)}) conditional(s32[]{:T(128)} %convert_element_type.92, () %tuple.70, (bf16[128,1536]{1,0:T(8,128)(2,1)S(1)}, f32[4608]{0:T(1024)}, bf16[1536,4608]{1,0:T(8,128)(2,1)}, f32[1,128]{1,0:T(1,128)S(1)}) %tuple.71), branch_computations={%region_2.2_spmd, %region_3.6_spmd} | conditional | flops 1815284864 | bytes 26018840 | solution.py:111
  933.0 7.2 fusion.6
  948.0 11.9 collective-permute-done
  962.1 24.4 %conditional.5 = (bf16[128,1536]{1,0:T(8,128)(2,1)}, bf16[1,128,1536]{2,1,0:T(8,128)(2,1)}) conditional(s32[]{:T(128)} %convert_element_type.92, () %tuple.69, (bf16[128,1536]{1,0:T(8,128)(2,1)S(1)}, f32[4608]{0:T(1024)}, bf16[4,128,3072]{2,1,0:T(8,128)(2,1)}, bf16[4,128,3072]{2,1,0:T(8,128)(2,1)}, f32[1,128]{1,0:T(1,128)S(1)}, ...), branch_computations={%region_7.7_spmd, %region_8.10_spmd} | conditional | flops 1443506688 | bytes 69053088 | solution.py:158
  965.3 4.7 copy.31
  970.0 5.6 pad_maximum_fusion
  977.2 3.3 bitcast_reduce_fusion
  989.8 10.3 collective-permute-done.1
  1007.0 13.7 %conditional.4 = (bf16[128,12,128]{0,2,1:T(8,128)(2,1)}, bf16[128,3072]{1,0:T(8,128)(2,1)}, bf16[1,128,3072]{2,1,0:T(8,128)(2,1)}) conditional(s32[]{:T(128)} %convert_element_type.92, () %tuple.70, (bf16[128,1536]{1,0:T(8,128)(2,1)S(1)}, f32[4608]{0:T(1024)}, bf16[1536,4608]{1,0:T(8,128)(2,1)}, f32[1,128]{1,0:T(1,128)S(1)}) %tuple.71), branch_computations={%region_2.2_spmd, %region_3.6_spmd} | conditional | flops 1815284864 | bytes 26018840 | solution.py:111
  1008.2 7.1 fusion.6
  1023.1 11.9 collective-permute-done
  1037.3 24.4 %conditional.5 = (bf16[128,1536]{1,0:T(8,128)(2,1)}, bf16[1,128,1536]{2,1,0:T(8,128)(2,1)}) conditional(s32[]{:T(128)} %convert_element_type.92, () %tuple.69, (bf16[128,1536]{1,0:T(8,128)(2,1)S(1)}, f32[4608]{0:T(1024)}, bf16[4,128,3072]{2,1,0:T(8,128)(2,1)}, bf16[4,128,3072]{2,1,0:T(8,128)(2,1)}, f32[1,128]{1,0:T(1,128)S(1)}, ...), branch_computations={%region_7.7_spmd, %region_8.10_spmd} | conditional | flops 1443506688 | bytes 69053088 | solution.py:158
  1040.5 4.7 copy.31
  1045.2 5.6 pad_maximum_fusion
  1052.3 3.3 bitcast_reduce_fusion
  1064.9 12.3 collective-permute-done.1
  1084.1 13.7 %conditional.4 = (bf16[128,12,128]{0,2,1:T(8,128)(2,1)}, bf16[128,3072]{1,0:T(8,128)(2,1)}, bf16[1,128,3072]{2,1,0:T(8,128)(2,1)}) conditional(s32[]{:T(128)} %convert_element_type.92, () %tuple.70, (bf16[128,1536]{1,0:T(8,128)(2,1)S(1)}, f32[4608]{0:T(1024)}, bf16[1536,4608]{1,0:T(8,128)(2,1)}, f32[1,128]{1,0:T(1,128)S(1)}) %tuple.71), branch_computations={%region_2.2_spmd, %region_3.6_spmd} | conditional | flops 1815284864 | bytes 26018840 | solution.py:111
  1085.3 7.1 fusion.6
  1100.2 11.9 collective-permute-done
  1114.4 24.4 %conditional.5 = (bf16[128,1536]{1,0:T(8,128)(2,1)}, bf16[1,128,1536]{2,1,0:T(8,128)(2,1)}) conditional(s32[]{:T(128)} %convert_element_type.92, () %tuple.69, (bf16[128,1536]{1,0:T(8,128)(2,1)S(1)}, f32[4608]{0:T(1024)}, bf16[4,128,3072]{2,1,0:T(8,128)(2,1)}, bf16[4,128,3072]{2,1,0:T(8,128)(2,1)}, f32[1,128]{1,0:T(1,128)S(1)}, ...), branch_computations={%region_7.7_spmd, %region_8.10_spmd} | conditional | flops 1443506688 | bytes 69053088 | solution.py:158
  1117.6 4.7 copy.31
  1122.3 5.6 pad_maximum_fusion
  1142.0 14.9 %collective-permute-done.1 = bf16[128,1536]{1,0:T(8,128)(2,1)S(1)} collective-permute-done((bf16[128,1536]{1,0:T(8,128)(2,1)}, bf16[128,1536]{1,0:T(8,128)(2,1)S(1)}, u32[]{:S(2)}, u32[]{:S(2)}) %collective-permute-start.1) | collective-permute-done | bytes 393248 | tf_op jit(solution)/shard_map/while/body/eval_jaxpr/ppermute | solution.py:34
  1163.8 13.7 %conditional.4 = (bf16[128,12,128]{0,2,1:T(8,128)(2,1)}, bf16[128,3072]{1,0:T(8,128)(2,1)}, bf16[1,128,3072]{2,1,0:T(8,128)(2,1)}) conditional(s32[]{:T(128)} %convert_element_type.92, () %tuple.70, (bf16[128,1536]{1,0:T(8,128)(2,1)S(1)}, f32[4608]{0:T(1024)}, bf16[1536,4608]{1,0:T(8,128)(2,1)}, f32[1,128]{1,0:T(1,128)S(1)}) %tuple.71), branch_computations={%region_2.2_spmd, %region_3.6_spmd} | conditional | flops 1815284864 | bytes 26018840 | solution.py:111
  1165.0 7.1 fusion.6
  1179.9 15.9 %collective-permute-done = bf16[128,3072]{1,0:T(8,128)(2,1)S(1)} collective-permute-done((bf16[128,3072]{1,0:T(8,128)(2,1)}, bf16[128,3072]{1,0:T(8,128)(2,1)S(1)}, u32[]{:S(2)}, u32[]{:S(2)}) %collective-permute-start) | collective-permute-done | bytes 786464 | tf_op jit(solution)/shard_map/while/body/eval_jaxpr/ppermute | solution.py:28
  1198.1 24.4 %conditional.5 = (bf16[128,1536]{1,0:T(8,128)(2,1)}, bf16[1,128,1536]{2,1,0:T(8,128)(2,1)}) conditional(s32[]{:T(128)} %convert_element_type.92, () %tuple.69, (bf16[128,1536]{1,0:T(8,128)(2,1)S(1)}, f32[4608]{0:T(1024)}, bf16[4,128,3072]{2,1,0:T(8,128)(2,1)}, bf16[4,128,3072]{2,1,0:T(8,128)(2,1)}, f32[1,128]{1,0:T(1,128)S(1)}, ...), branch_computations={%region_7.7_spmd, %region_8.10_spmd} | conditional | flops 1443506688 | bytes 69053088 | solution.py:158
  1201.2 4.7 copy.31
  1205.9 5.6 pad_maximum_fusion
  (276 shorter events, 281.7 us)
Async XLA Ops:
  7.2 3.8 copy-start
  17.7 13.5 %copy-start.1 = (f32[1,16,3,1536]{3,1,2,0:T(8,128)S(1)}, f32[1,16,3,1536]{3,1,2,0:T(8,128)}, u32[]{:S(2)}) copy-start(f32[1,16,3,1536]{3,1,2,0:T(8,128)} %param.22) | copy-start | bytes 884740
  17.7 420.7 %all-to-all-start = ((bf16[32,48,4608]{2,1,0:T(8,128)(2,1)}), bf16[32,48,4608]{2,1,0:T(8,128)(2,1)}, u32[]{:S(2)}, u32[]{:S(2)}) async-start(bf16[32,48,4608]{2,1,0:T(8,128)(2,1)} %tile.9), calls=%async_computation | async-start | bytes 28311552 | tf_op jit(solution)/shard_map/all_to_all | solution.py:20
  29.2 410.6 %copy-start.2 = (f32[1,128]{1,0:T(1,128)S(1)}, f32[1,128]{1,0:T(1,128)}, u32[]{:S(2)}) copy-start(f32[1,128]{1,0:T(1,128)} %param.20) | copy-start | bytes 1540
  29.2 410.6 %copy-start.3 = (s32[4]{0:T(128)S(1)}, s32[4]{0:T(128)}, u32[]{:S(2)}) copy-start(s32[4]{0:T(128)} %param.25) | copy-start | bytes 52
  29.2 410.5 %copy-start.4 = (s32[4]{0:T(128)S(1)}, s32[4]{0:T(128)}, u32[]{:S(2)}) copy-start(s32[4]{0:T(128)} %param.24) | copy-start | bytes 52
  29.2 410.5 %copy-start.5 = (f32[1,128]{1,0:T(1,128)S(1)}, f32[1,128]{1,0:T(1,128)}, u32[]{:S(2)}) copy-start(f32[1,128]{1,0:T(1,128)} %param.21) | copy-start | bytes 1540
  29.2 409.2 %all-gather.3.cloned.1.call-start = ((), (), s32[]{:S(2)}) async-start(), calls=%async_computation.1 | async-start | bytes 4866048 | tf_op jit(solution)/shard_map/all_gather | solution.py:59
  29.9 408.5 %collective-permute-start.2 = (bf16[4,128,3072]{2,1,0:T(8,128)(2,1)}, bf16[4,128,3072]{2,1,0:T(8,128)(2,1)}, u32[]{:S(2)}, u32[]{:S(2)}) collective-permute-start(bf16[4,128,3072]{2,1,0:T(8,128)(2,1)} %bitcast.20), channel_id=1, source_target_pairs={{0,1},{1,2},{2,3},{3,4},{4,5},{5,6},{6,7},{7,8},{8,9},{9,10},{10,1... | collective-permute-start | bytes 9437192 | tf_op jit(solution)/shard_map/ppermute | solution.py:28
  449.7 21.1 %collective-permute-start = (bf16[128,3072]{1,0:T(8,128)(2,1)}, bf16[128,3072]{1,0:T(8,128)(2,1)S(1)}, u32[]{:S(2)}, u32[]{:S(2)}) collective-permute-start(bf16[128,3072]{1,0:T(8,128)(2,1)} %get-tuple-element.585), channel_id=1, source_target_pairs={{0,1},{1,2},{2,3},{3,4},{4,5},{5,6},{6,7},{7,8},{8,9},{9,10},{10,1... | collective-permute-start | bytes 2359304 | tf_op jit(solution)/shard_map/while/body/eval_jaxpr/ppermute | solution.py:28
  474.6 5.7 collective-permute-start.1
  490.0 16.0 %collective-permute-start = (bf16[128,3072]{1,0:T(8,128)(2,1)}, bf16[128,3072]{1,0:T(8,128)(2,1)S(1)}, u32[]{:S(2)}, u32[]{:S(2)}) collective-permute-start(bf16[128,3072]{1,0:T(8,128)(2,1)} %get-tuple-element.585), channel_id=1, source_target_pairs={{0,1},{1,2},{2,3},{3,4},{4,5},{5,6},{6,7},{7,8},{8,9},{9,10},{10,1... | collective-permute-start | bytes 2359304 | tf_op jit(solution)/shard_map/while/body/eval_jaxpr/ppermute | solution.py:28
  509.8 17.6 %collective-permute-start.1 = (bf16[128,1536]{1,0:T(8,128)(2,1)}, bf16[128,1536]{1,0:T(8,128)(2,1)S(1)}, u32[]{:S(2)}, u32[]{:S(2)}) collective-permute-start(bf16[128,1536]{1,0:T(8,128)(2,1)} %get-tuple-element.587), channel_id=1, source_target_pairs={{0,32},{32,64},{64,96},{96,128},{128,160},{160,192},{192,224},{1,3... | collective-permute-start | bytes 1179656 | tf_op jit(solution)/shard_map/while/body/eval_jaxpr/ppermute | solution.py:34
  537.2 16.4 %collective-permute-start = (bf16[128,3072]{1,0:T(8,128)(2,1)}, bf16[128,3072]{1,0:T(8,128)(2,1)S(1)}, u32[]{:S(2)}, u32[]{:S(2)}) collective-permute-start(bf16[128,3072]{1,0:T(8,128)(2,1)} %get-tuple-element.585), channel_id=1, source_target_pairs={{0,1},{1,2},{2,3},{3,4},{4,5},{5,6},{6,7},{7,8},{8,9},{9,10},{10,1... | collective-permute-start | bytes 2359304 | tf_op jit(solution)/shard_map/while/body/eval_jaxpr/ppermute | solution.py:28
  557.3 10.4 collective-permute-start.1
  577.5 16.6 %collective-permute-start = (bf16[128,3072]{1,0:T(8,128)(2,1)}, bf16[128,3072]{1,0:T(8,128)(2,1)S(1)}, u32[]{:S(2)}, u32[]{:S(2)}) collective-permute-start(bf16[128,3072]{1,0:T(8,128)(2,1)} %get-tuple-element.585), channel_id=1, source_target_pairs={{0,1},{1,2},{2,3},{3,4},{4,5},{5,6},{6,7},{7,8},{8,9},{9,10},{10,1... | collective-permute-start | bytes 2359304 | tf_op jit(solution)/shard_map/while/body/eval_jaxpr/ppermute | solution.py:28
  597.9 10.2 collective-permute-start.1
  617.8 16.6 %collective-permute-start = (bf16[128,3072]{1,0:T(8,128)(2,1)}, bf16[128,3072]{1,0:T(8,128)(2,1)S(1)}, u32[]{:S(2)}, u32[]{:S(2)}) collective-permute-start(bf16[128,3072]{1,0:T(8,128)(2,1)} %get-tuple-element.585), channel_id=1, source_target_pairs={{0,1},{1,2},{2,3},{3,4},{4,5},{5,6},{6,7},{7,8},{8,9},{9,10},{10,1... | collective-permute-start | bytes 2359304 | tf_op jit(solution)/shard_map/while/body/eval_jaxpr/ppermute | solution.py:28
  638.2 10.2 collective-permute-start.1
  658.1 16.6 %collective-permute-start = (bf16[128,3072]{1,0:T(8,128)(2,1)}, bf16[128,3072]{1,0:T(8,128)(2,1)S(1)}, u32[]{:S(2)}, u32[]{:S(2)}) collective-permute-start(bf16[128,3072]{1,0:T(8,128)(2,1)} %get-tuple-element.585), channel_id=1, source_target_pairs={{0,1},{1,2},{2,3},{3,4},{4,5},{5,6},{6,7},{7,8},{8,9},{9,10},{10,1... | collective-permute-start | bytes 2359304 | tf_op jit(solution)/shard_map/while/body/eval_jaxpr/ppermute | solution.py:28
  678.5 10.2 collective-permute-start.1
  698.5 14.4 %collective-permute-start = (bf16[128,3072]{1,0:T(8,128)(2,1)}, bf16[128,3072]{1,0:T(8,128)(2,1)S(1)}, u32[]{:S(2)}, u32[]{:S(2)}) collective-permute-start(bf16[128,3072]{1,0:T(8,128)(2,1)} %get-tuple-element.585), channel_id=1, source_target_pairs={{0,1},{1,2},{2,3},{3,4},{4,5},{5,6},{6,7},{7,8},{8,9},{9,10},{10,1... | collective-permute-start | bytes 2359304 | tf_op jit(solution)/shard_map/while/body/eval_jaxpr/ppermute | solution.py:28
  716.6 208.3 %collective-permute-start.1 = (bf16[128,1536]{1,0:T(8,128)(2,1)}, bf16[128,1536]{1,0:T(8,128)(2,1)S(1)}, u32[]{:S(2)}, u32[]{:S(2)}) collective-permute-start(bf16[128,1536]{1,0:T(8,128)(2,1)} %get-tuple-element.587), channel_id=1, source_target_pairs={{0,32},{32,64},{64,96},{96,128},{128,160},{160,192},{192,224},{1,3... | collective-permute-start | bytes 1179656 | tf_op jit(solution)/shard_map/while/body/eval_jaxpr/ppermute | solution.py:34
  945.5 14.4 %collective-permute-start = (bf16[128,3072]{1,0:T(8,128)(2,1)}, bf16[128,3072]{1,0:T(8,128)(2,1)S(1)}, u32[]{:S(2)}, u32[]{:S(2)}) collective-permute-start(bf16[128,3072]{1,0:T(8,128)(2,1)} %get-tuple-element.585), channel_id=1, source_target_pairs={{0,1},{1,2},{2,3},{3,4},{4,5},{5,6},{6,7},{7,8},{8,9},{9,10},{10,1... | collective-permute-start | bytes 2359304 | tf_op jit(solution)/shard_map/while/body/eval_jaxpr/ppermute | solution.py:28
  977.2 6.0 slice-start
  980.5 2.7 slice-start.1
  986.5 13.5 %collective-permute-start.1 = (bf16[128,1536]{1,0:T(8,128)(2,1)}, bf16[128,1536]{1,0:T(8,128)(2,1)S(1)}, u32[]{:S(2)}, u32[]{:S(2)}) collective-permute-start(bf16[128,1536]{1,0:T(8,128)(2,1)} %get-tuple-element.587), channel_id=1, source_target_pairs={{0,32},{32,64},{64,96},{96,128},{128,160},{160,192},{192,224},{1,3... | collective-permute-start | bytes 1179656 | tf_op jit(solution)/shard_map/while/body/eval_jaxpr/ppermute | solution.py:34
  1020.7 14.4 %collective-permute-start = (bf16[128,3072]{1,0:T(8,128)(2,1)}, bf16[128,3072]{1,0:T(8,128)(2,1)S(1)}, u32[]{:S(2)}, u32[]{:S(2)}) collective-permute-start(bf16[128,3072]{1,0:T(8,128)(2,1)} %get-tuple-element.585), channel_id=1, source_target_pairs={{0,1},{1,2},{2,3},{3,4},{4,5},{5,6},{6,7},{7,8},{8,9},{9,10},{10,1... | collective-permute-start | bytes 2359304 | tf_op jit(solution)/shard_map/while/body/eval_jaxpr/ppermute | solution.py:28
  1052.3 6.0 slice-start
  1055.6 2.7 slice-start.1
  1061.7 15.5 %collective-permute-start.1 = (bf16[128,1536]{1,0:T(8,128)(2,1)}, bf16[128,1536]{1,0:T(8,128)(2,1)S(1)}, u32[]{:S(2)}, u32[]{:S(2)}) collective-permute-start(bf16[128,1536]{1,0:T(8,128)(2,1)} %get-tuple-element.587), channel_id=1, source_target_pairs={{0,32},{32,64},{64,96},{96,128},{128,160},{160,192},{192,224},{1,3... | collective-permute-start | bytes 1179656 | tf_op jit(solution)/shard_map/while/body/eval_jaxpr/ppermute | solution.py:34
  1097.8 14.4 %collective-permute-start = (bf16[128,3072]{1,0:T(8,128)(2,1)}, bf16[128,3072]{1,0:T(8,128)(2,1)S(1)}, u32[]{:S(2)}, u32[]{:S(2)}) collective-permute-start(bf16[128,3072]{1,0:T(8,128)(2,1)} %get-tuple-element.585), channel_id=1, source_target_pairs={{0,1},{1,2},{2,3},{3,4},{4,5},{5,6},{6,7},{7,8},{8,9},{9,10},{10,1... | collective-permute-start | bytes 2359304 | tf_op jit(solution)/shard_map/while/body/eval_jaxpr/ppermute | solution.py:28
  1129.4 6.0 slice-start
  1132.7 2.7 slice-start.1
  1138.8 18.1 %collective-permute-start.1 = (bf16[128,1536]{1,0:T(8,128)(2,1)}, bf16[128,1536]{1,0:T(8,128)(2,1)S(1)}, u32[]{:S(2)}, u32[]{:S(2)}) collective-permute-start(bf16[128,1536]{1,0:T(8,128)(2,1)} %get-tuple-element.587), channel_id=1, source_target_pairs={{0,32},{32,64},{64,96},{96,128},{128,160},{160,192},{192,224},{1,3... | collective-permute-start | bytes 1179656 | tf_op jit(solution)/shard_map/while/body/eval_jaxpr/ppermute | solution.py:34
  1177.5 18.3 %collective-permute-start = (bf16[128,3072]{1,0:T(8,128)(2,1)}, bf16[128,3072]{1,0:T(8,128)(2,1)S(1)}, u32[]{:S(2)}, u32[]{:S(2)}) collective-permute-start(bf16[128,3072]{1,0:T(8,128)(2,1)} %get-tuple-element.585), channel_id=1, source_target_pairs={{0,1},{1,2},{2,3},{3,4},{4,5},{5,6},{6,7},{7,8},{8,9},{9,10},{10,1... | collective-permute-start | bytes 2359304 | tf_op jit(solution)/shard_map/while/body/eval_jaxpr/ppermute | solution.py:28
  1213.1 6.0 slice-start
  1216.4 2.7 slice-start.1
  1222.5 3.8 collective-permute-start.1
Sparse Core Ops, SparseCore 0:
  32.6 156.9 all-gather.2
